TPU v7x, 32 devices: a whole 2x2x4 slice. The times are simulated.
32 devices in a mesh: dp: 2 (over y), table: 16 (over z, x, core).
Axes of the slice: x: 2, y: 2, z: 4, core: 2. Of those that a mesh axis runs over, the one named last changes fastest.
Arguments:
- gradients: bfloat16 [256, 4096], P(None, ('dp', 'table')), may hold values from -16 to 16
- row_ids: int32 [4096], P(('dp', 'table')), may hold values from 0 to 32767
- table_block: float32 [256, 32768], P('table', 'dp'), may hold values from -6 to 6
- adagrad_state: float32 [32768], P('dp'), may hold values from 0.05 to 2
Outputs:
- new_table: float32 [256, 32768], P('table', 'dp')
- new_state: float32 [32768], P('dp')
All inputs are finite; a program needn't handle non-finite values.
Results may differ from a plain program's by a relative error of at most 0.0003.
Values may be sent and summed in bfloat16 or wider, within the bound.
A program may use at most 64 MiB of HBM per device.

v0:
```python
import functools

import jax
import jax.numpy as jnp
from jax import lax
from jax.experimental import pallas as pl
from jax.experimental.pallas import tpu as pltpu
from jax.sharding import PartitionSpec as P

learn_rate = 0.5
LO = 256
LANES = 128
GROUP = 4
PIECES = 4
MESH = pl.DeviceIdType.MESH


def accumulate(grads, ids, first_row, count_rows):
    relative = ids - first_row
    inside = (relative >= 0) & (relative < count_rows)
    target = jnp.where(inside, relative, count_rows)
    start_total = jnp.zeros((grads.shape[0], count_rows), jnp.float32)
    return start_total.at[:, target].add(grads.astype(jnp.float32), mode="drop")


def plain_body(width, gradients, row_ids, table_block, adagrad_state):
    owned = lax.all_to_all(gradients, "table", split_axis=0, concat_axis=1, tiled=True)
    local_rows = table_block.shape[1]
    all_row_ids = lax.all_gather(row_ids, ("dp", "table"), axis=0, tiled=True)
    first_row = lax.axis_index("dp") * local_rows
    row_grad = accumulate(
        lax.all_gather(owned, "dp", axis=1, tiled=True), all_row_ids, first_row, local_rows
    )
    partial_squares = jnp.sum(row_grad * row_grad, axis=0)
    squares = lax.psum(partial_squares, "table")
    new_state = adagrad_state + squares / width
    new_table = table_block - learn_rate * row_grad / jnp.sqrt(new_state)[None, :]
    return (new_table, new_state)


def flips(value, size):
    table, bit = [value], 1
    while bit < size:
        change = bit - 2 * bit * lax.rem(value // bit, 2)
        table = table + [old + change for old in table]
        bit *= 2
    return table


def exchange_kernel(
    dp, tb, cols, rows, width,
    g_ref, id_ref, state_ref, table_ref, table_out, state_out,
    acc, got_g, got_i, near_g, near_i, table, part, red, total, full, state,
    send_g, send_i, send_r, send_a, recv_g, recv_i, recv_r, recv_a, own_sem,
):
    d, t = lax.axis_index("dp"), lax.axis_index("table")
    n = dp * tb
    me = d * tb + t
    his = rows // LO
    teams = tb
    base = 0
    lines = rows // teams // LANES
    parts = LO // LANES
    each = his // teams
    first_row = d * rows
    ts, ds = flips(t, tb), flips(d, dp)
    reducer = jnp.logical_and(t >= base, t < base + teams)

    def device(k):
        return ds[k // 4 % dp], ts[k % 4 + k // (4 * dp) * 4]

    barrier = pltpu.get_barrier_semaphore()
    for k in reversed(range(1, n)):
        pl.semaphore_signal(barrier, inc=1, device_id=device(k), device_id_type=MESH)

    own = (
        pltpu.make_async_copy(g_ref, near_g, own_sem.at[0]),
        pltpu.make_async_copy(id_ref, near_i, own_sem.at[1]),
        pltpu.make_async_copy(state_ref, state, own_sem.at[2]),
        pltpu.make_async_copy(table_ref, table, own_sem.at[3]),
    )
    for copy in own:
        copy.start()
    acc[...] = jnp.zeros_like(acc)
    own[0].wait()
    own[1].wait()
    got_g[me] = near_g[t]
    got_i[me] = near_i[...]
    pl.semaphore_wait(barrier, n - 1)

    def block_copies(k):
        to = device(k)
        return (
            pltpu.make_async_remote_copy(
                src_ref=near_i, dst_ref=got_i.at[me],
                send_sem=send_i.at[k], recv_sem=recv_i.at[k],
                device_id=to, device_id_type=MESH,
            ),
            pltpu.make_async_remote_copy(
                src_ref=near_g.at[to[1]], dst_ref=got_g.at[me],
                send_sem=send_g.at[k], recv_sem=recv_g.at[k],
                device_id=to, device_id_type=MESH,
            ),
        )

    for k in range(1, n):
        for copy in block_copies(k):
            copy.start()

    def arrived(k):
        there = device(k)
        source = there[0] * tb + there[1]
        pltpu.make_async_copy(near_i, got_i.at[source], recv_i.at[k]).wait()
        pltpu.make_async_copy(near_g.at[t], got_g.at[source], recv_g.at[k]).wait()
        return source

    def add(sources):
        ids = jnp.concatenate([got_i[k] for k in sources], axis=1) - first_row
        grads = jnp.concatenate([got_g[k] for k in sources], axis=1)
        span = ids.shape[1]
        low = jnp.broadcast_to(lax.bitwise_and(ids, LO - 1), (LO, span))
        place = lax.broadcasted_iota(jnp.int32, (LO, span), 0)
        one_hot = jnp.where(low == place, 1.0, 0.0).astype(jnp.bfloat16)
        high = jnp.broadcast_to(lax.shift_right_arithmetic(ids, 8), (cols, span))
        high = jnp.clip(high, -1, his).astype(jnp.float32).astype(jnp.bfloat16)
        zero = jnp.zeros_like(grads)
        picked = jnp.concatenate(
            [jnp.where(high == jnp.bfloat16(h), grads, zero) for h in range(his)], axis=0
        )
        acc[...] += lax.dot_general(
            picked, one_hot, (((1,), (1,)), ((), ())), preferred_element_type=jnp.float32
        )

    add([me] + [arrived(k) for k in range(1, GROUP)])
    for first in range(GROUP, n, GROUP):
        add([arrived(k) for k in range(first, first + GROUP)])

    for j in range(teams):
        pieces = []
        for h in range(each):
            at = (j * each + h) * cols
            piece = acc[at:at + cols, :]
            sums = jnp.sum(piece * piece, axis=0, keepdims=True)
            for half in range(parts):
                pieces.append(sums[:, half * LANES:(half + 1) * LANES])
        part[j] = jnp.concatenate(pieces, axis=0)

    def part_copy(k):
        team = ts[k]
        return pltpu.make_async_remote_copy(
            src_ref=part.at[team], dst_ref=red.at[t],
            send_sem=send_r.at[k], recv_sem=recv_r.at[t],
            device_id=(d, team + base), device_id_type=MESH,
        )

    for k in reversed(range(1, teams)):
        part_copy(k).start()

    own[2].wait()
    own[3].wait()

    def total_copy(k):
        return pltpu.make_async_remote_copy(
            src_ref=total, dst_ref=full.at[t - base],
            send_sem=send_a.at[k], recv_sem=recv_a.at[t - base],
            device_id=(d, ts[k]), device_id_type=MESH,
        )

    @pl.when(reducer)
    def _():
        mine = t - base
        red[t] = part[mine]
        for k in range(1, tb):
            pltpu.make_async_copy(part.at[0], red.at[ts[k]], recv_r.at[ts[k]]).wait()
        here = pl.ds(pl.multiple_of(mine * lines, lines), lines)
        fresh = state[here, :] + jnp.sum(red[...], axis=0) / width
        total[...] = fresh
        full[mine] = fresh
        for k in range(1, teams):
            part_copy(k).wait_send()
        for k in reversed(range(1, tb)):
            total_copy(k).start()

    def update(j):
        fresh = full[j]
        state_out[j] = fresh
        scale = learn_rate / jnp.sqrt(fresh)
        for r in range(lines):
            h, half = r // parts, r % parts
            at = pl.multiple_of((j * each + h) * cols, cols)
            lanes = pl.ds(pl.multiple_of((j * lines + r) * LANES, LANES), LANES)
            step = acc[pl.ds(at, cols), half * LANES:(half + 1) * LANES]
            table_out[:, lanes] = table[:, lanes] - step * scale[r:r + 1, :]

    for k in range(1, n):
        for copy in block_copies(k):
            copy.wait_send()

    def receive(k):
        team = lax.rem(t + (tb - base + k), teams)
        pltpu.make_async_copy(total, full.at[team], recv_a.at[team]).wait()
        update(team)

    @pl.when(reducer)
    def _():
        update(t - base)

    @pl.loop(1, teams)
    def _(k):
        receive(k)

    @pl.when(reducer)
    def _():
        for k in range(1, tb):
            total_copy(k).wait_send()


def finish_kernel(table_ref, state_ref, table_out, state_out, sems):
    rows = table_ref.shape[1]
    size = rows // PIECES
    copies = [
        pltpu.make_async_copy(
            table_ref.at[:, pl.ds(p * size, size)], table_out.at[:, pl.ds(p * size, size)], sems.at[p]
        )
        for p in range(PIECES)
    ]
    copies.append(pltpu.make_async_copy(state_ref, state_out, sems.at[PIECES]))
    for copy in copies:
        copy.start()
    for copy in copies:
        copy.wait()


def kernel_body(dp, tb, width, gradients, row_ids, table_block, adagrad_state):
    cols, rows = table_block.shape
    count = row_ids.shape[0]
    n = dp * tb
    his = rows // LO
    teams = tb
    lines = rows // teams // LANES
    dma = pltpu.SemaphoreType.DMA
    new_table, new_state = pl.pallas_call(
        functools.partial(exchange_kernel, dp, tb, cols, rows, width),
        name="exchange",
        out_shape=(
            pltpu.VMEM((cols, rows), jnp.float32),
            pltpu.VMEM((teams, lines, LANES), jnp.float32),
        ),
        in_specs=[pl.BlockSpec(memory_space=pl.ANY)] * 4,
        out_specs=(pl.BlockSpec(memory_space=pltpu.VMEM),) * 2,
        scratch_shapes=[
            pltpu.VMEM((his * cols, LO), jnp.float32),
            pltpu.VMEM((n, cols, count), jnp.bfloat16),
            pltpu.VMEM((n, 1, count), jnp.int32),
            pltpu.VMEM((tb, cols, count), jnp.bfloat16),
            pltpu.VMEM((1, count), jnp.int32),
            pltpu.VMEM((cols, rows), jnp.float32),
            pltpu.VMEM((teams, lines, LANES), jnp.float32),
            pltpu.VMEM((tb, lines, LANES), jnp.float32),
            pltpu.VMEM((lines, LANES), jnp.float32),
            pltpu.VMEM((teams, lines, LANES), jnp.float32),
            pltpu.VMEM((rows // LANES, LANES), jnp.float32),
            dma((n,)), dma((n,)), dma((teams,)), dma((tb,)),
            dma((n,)), dma((n,)), dma((tb,)), dma((teams,)),
            dma((4,)),
        ],
        compiler_params=pltpu.CompilerParams(collective_id=0, has_side_effects=True),
    )(
        gradients.reshape(tb, cols, count),
        row_ids.reshape(1, count),
        adagrad_state.reshape(rows // LANES, LANES),
        table_block,
    )
    new_table, new_state = pl.pallas_call(
        finish_kernel,
        name="finish",
        out_shape=(
            jax.ShapeDtypeStruct((cols, rows), jnp.float32),
            jax.ShapeDtypeStruct((teams, lines, LANES), jnp.float32),
        ),
        in_specs=[pl.BlockSpec(memory_space=pltpu.VMEM)] * 2,
        out_specs=(pl.BlockSpec(memory_space=pl.ANY),) * 2,
        scratch_shapes=[dma((PIECES + 1,))],
    )(
        pltpu.with_memory_space_constraint(new_table, pltpu.VMEM),
        pltpu.with_memory_space_constraint(new_state, pltpu.VMEM),
    )
    return (new_table, new_state.reshape(rows))


def body(dp, tb, gradients, row_ids, table_block, adagrad_state):
    width = gradients.shape[0]
    cols, rows = table_block.shape
    fits = (
        cols % 16 == 0
        and rows % (tb * 8 * LANES) == 0
        and rows % (4 * LO * 4) == 0
        and dp & (dp - 1) == 0
        and tb & (tb - 1) == 0
        and tb % 4 == 0
        and rows // LO <= 256
        and row_ids.shape[0] == LANES
    )
    args = (gradients, row_ids, table_block, adagrad_state)
    if fits:
        return kernel_body(dp, tb, width, *args)
    return plain_body(width, *args)


def solution(mesh):
    in_specs = (P(None, ("dp", "table")), P(("dp", "table")), P("table", "dp"), P("dp"))
    out_specs = (P("table", "dp"), P("dp"))
    run = functools.partial(body, mesh.shape["dp"], mesh.shape["table"])
    return jax.shard_map(run, mesh=mesh, in_specs=in_specs, out_specs=out_specs, check_vma=False)
```

profile of v0, /device:TPU:0, one launch (start us, length us, event | category | flops | bytes accessed | tf_op | source)
XLA Modules:
  0.0 26.1 jit_solution(11499523924378066023)
XLA Ops:
  0.6 24.5 %exchange.1 = (f32[16,16384]{1,0:T(8,128)S(1)}, f32[16,8,128]{2,1,0:T(8,128)S(1)}) custom-call(bf16[16,16,128]{2,1,0:T(8,128)(2,1)} %bitcast.4, s32[1,128]{1,0:T(1,128)} %bitcast.6, f32[128,128]{1,0:T(8,128)} %bitcast.5, f32[16,16384]{1,0:T(8,128)} %table_ref.1), custom_call_target="tpu_custom_call" | custom-call | tf_op jit(solution)/shard_map/exchange/pallas_call | solution.py:242
  25.1 1.0 %finish.1 = (f32[16,16384]{1,0:T(8,128)}, f32[16,8,128]{2,1,0:T(8,128)}) custom-call(f32[16,16384]{1,0:T(8,128)S(1)} %get-tuple-element.6.table_ref, f32[16,8,128]{2,1,0:T(8,128)S(1)} %get-tuple-element.7.state_ref), custom_call_target="tpu_custom_call" | custom-call | tf_op jit(solution)/shard_map/finish/pallas_call | solution.py:274
where the time goes:
time: 26.3 us; the launch traced here: 26.1 us
  Pallas kernels  25.5 us (97%)
  between operations  0.64 us (2%)
    pallas_call x1, Pallas kernels, kernel_body(): pl.pallas_call(functools.partial(exchange_kernel, dp, tb, cols, rows, wid...  24.5 us
    pallas_call x1, Pallas kernels, kernel_body(): pl.pallas_call(finish_kernel, name='finish', out_shape=(jax.ShapeDtypeStr...  1.02 us

commit v1 on v0

v1 whole, which is shorter than its diff:
```python
import functools

import jax
import jax.numpy as jnp
from jax import lax
from jax.experimental import pallas as pl
from jax.experimental.pallas import tpu as pltpu
from jax.sharding import PartitionSpec as P

learn_rate = 0.5
LO = 256
LANES = 128
GROUP = 4
READY = 2
PIECES = 4
MESH = pl.DeviceIdType.MESH


def accumulate(grads, ids, first_row, count_rows):
    relative = ids - first_row
    inside = (relative >= 0) & (relative < count_rows)
    target = jnp.where(inside, relative, count_rows)
    start_total = jnp.zeros((grads.shape[0], count_rows), jnp.float32)
    return start_total.at[:, target].add(grads.astype(jnp.float32), mode="drop")


def plain_body(width, gradients, row_ids, table_block, adagrad_state):
    owned = lax.all_to_all(gradients, "table", split_axis=0, concat_axis=1, tiled=True)
    local_rows = table_block.shape[1]
    all_row_ids = lax.all_gather(row_ids, ("dp", "table"), axis=0, tiled=True)
    first_row = lax.axis_index("dp") * local_rows
    row_grad = accumulate(
        lax.all_gather(owned, "dp", axis=1, tiled=True), all_row_ids, first_row, local_rows
    )
    partial_squares = jnp.sum(row_grad * row_grad, axis=0)
    squares = lax.psum(partial_squares, "table")
    new_state = adagrad_state + squares / width
    new_table = table_block - learn_rate * row_grad / jnp.sqrt(new_state)[None, :]
    return (new_table, new_state)


def flips(value, size):
    table, bit = [value], 1
    while bit < size:
        change = bit - 2 * bit * lax.rem(value // bit, 2)
        table = table + [old + change for old in table]
        bit *= 2
    return table


def ready_groups(chips):
    groups, first = [], 1
    while first < chips:
        size = min(first, READY)
        groups.append(range(first, first + size))
        first += size
    return groups


def exchange_kernel(
    dp, tb, cols, rows, width,
    g_ref, id_ref, state_ref, table_ref, table_out, state_out,
    acc, pair_g, pair_i, got_g, got_i, table, part, red, total, full, state,
    send_g, send_i, send_r, send_a, recv_g, recv_i, recv_r, recv_a, own_sem, ready,
):
    d, t = lax.axis_index("dp"), lax.axis_index("table")
    chips = dp * tb // 2
    his = rows // LO
    lines = rows // tb // LANES
    parts = LO // LANES
    each = his // tb
    first_row = d * rows
    ts, ds = flips(t, tb), flips(d, dp)
    core, spot = lax.rem(t, 2), t // 2
    order = t // 4 * (2 * dp) + d * 2 + lax.rem(spot, 2)
    groups = ready_groups(chips)
    sibling = (d, ts[1])

    def device(m):
        return ds[m // 2 % dp], ts[m % 2 * 2 + m // (2 * dp) * 4]

    def earlier(group):
        top = 1
        while top * 2 <= group[0]:
            top *= 2
        return lax.rem(order // top, 2) == 1

    def signal(semaphore, to):
        pl.semaphore_signal(semaphore, inc=1, device_id=to, device_id_type=MESH)

    def wait_blocks(ref, sem, count):
        there = ref.at[pl.ds(0, count)]
        pltpu.make_async_copy(there, there, sem).wait()

    barrier = pltpu.get_barrier_semaphore()

    @pl.when(core == 0)
    def _():
        signal(barrier, sibling)

    for group in reversed(groups):
        @pl.when(jnp.logical_not(earlier(group)))
        def _(group=group):
            for m in group:
                signal(barrier, device(m))

    own = (
        pltpu.make_async_copy(g_ref.at[:, core], pair_g.at[:, core], own_sem.at[0]),
        pltpu.make_async_copy(id_ref, pair_i.at[core], own_sem.at[1]),
        pltpu.make_async_copy(state_ref, state, own_sem.at[2]),
        pltpu.make_async_copy(table_ref, table, own_sem.at[3]),
    )
    own[0].start()
    own[1].start()

    @pl.when(order + core > 0)
    def _():
        pl.semaphore_wait(barrier, order + core)

    @pl.when(core == 1)
    def _():
        signal(ready.at[0], sibling)

    for g, group in reversed(list(enumerate(groups))):
        @pl.when(earlier(group))
        def _(g=g, group=group):
            for m in group:
                signal(ready.at[g + 1], device(m))

    @pl.when(core == 0)
    def _():
        pl.semaphore_wait(ready.at[0], 1)

    pltpu.make_async_remote_copy(
        src_ref=id_ref, dst_ref=pair_i.at[core],
        send_sem=send_i.at[0], recv_sem=recv_i.at[0],
        device_id=sibling, device_id_type=MESH,
    ).start()
    pltpu.make_async_remote_copy(
        src_ref=g_ref.at[:, 1 - core], dst_ref=pair_g.at[:, core],
        send_sem=send_g.at[0], recv_sem=recv_g.at[0],
        device_id=sibling, device_id_type=MESH,
    ).start()
    own[2].start()
    own[3].start()
    own[0].wait()
    own[1].wait()
    pltpu.make_async_copy(id_ref, pair_i.at[1 - core], recv_i.at[0]).wait()
    pltpu.make_async_copy(g_ref.at[:, 0], pair_g.at[:, 1 - core], recv_g.at[0]).wait()

    def send(m):
        to = device(m)
        pltpu.make_async_remote_copy(
            src_ref=pair_i, dst_ref=got_i.at[m],
            send_sem=send_i.at[1], recv_sem=recv_i.at[1 + m // GROUP],
            device_id=to, device_id_type=MESH,
        ).start()
        pltpu.make_async_remote_copy(
            src_ref=pair_g.at[to[1] // 2], dst_ref=got_g.at[m],
            send_sem=send_g.at[1], recv_sem=recv_g.at[1 + m // GROUP],
            device_id=to, device_id_type=MESH,
        ).start()

    for group in reversed(groups):
        @pl.when(earlier(group))
        def _(group=group):
            for m in reversed(group):
                send(m)

    acc[...] = jnp.zeros_like(acc)
    got_g[0] = pair_g[spot]
    got_i[0] = pair_i[...]

    for g, group in enumerate(groups):
        @pl.when(jnp.logical_not(earlier(group)))
        def _(g=g, group=group):
            pl.semaphore_wait(ready.at[g + 1], len(group))
            for m in group:
                send(m)

    def add(sources):
        both = [(m, c) for m in sources for c in range(2)]
        ids = jnp.concatenate([got_i[m, c] for m, c in both], axis=1) - first_row
        grads = jnp.concatenate([got_g[m, c] for m, c in both], axis=1)
        span = ids.shape[1]
        low = jnp.broadcast_to(lax.bitwise_and(ids, LO - 1), (LO, span))
        place = lax.broadcasted_iota(jnp.int32, (LO, span), 0)
        one_hot = jnp.where(low == place, 1.0, 0.0).astype(jnp.bfloat16)
        high = jnp.broadcast_to(lax.shift_right_arithmetic(ids, 8), (cols, span))
        high = jnp.clip(high, -1, his).astype(jnp.float32).astype(jnp.bfloat16)
        zero = jnp.zeros_like(grads)
        picked = jnp.concatenate(
            [jnp.where(high == jnp.bfloat16(h), grads, zero) for h in range(his)], axis=0
        )
        acc[...] += lax.dot_general(
            picked, one_hot, (((1,), (1,)), ((), ())), preferred_element_type=jnp.float32
        )

    for first in range(0, chips, GROUP):
        count = GROUP if first else GROUP - 1
        wait_blocks(got_i, recv_i.at[1 + first // GROUP], count)
        wait_blocks(got_g, recv_g.at[1 + first // GROUP], count)
        add(range(first, first + GROUP))

    for j in range(tb):
        pieces = []
        for h in range(each):
            at = (j * each + h) * cols
            piece = acc[at:at + cols, :]
            sums = jnp.sum(piece * piece, axis=0, keepdims=True)
            for half in range(parts):
                pieces.append(sums[:, half * LANES:(half + 1) * LANES])
        part[j] = jnp.concatenate(pieces, axis=0)

    for k in reversed(range(1, tb)):
        pltpu.make_async_remote_copy(
            src_ref=part.at[ts[k]], dst_ref=red.at[k],
            send_sem=send_r.at[0], recv_sem=recv_r.at[0],
            device_id=(d, ts[k]), device_id_type=MESH,
        ).start()
    red[0] = part[t]

    own[2].wait()
    own[3].wait()

    wait_blocks(red, recv_r.at[0], tb - 1)
    here = pl.ds(pl.multiple_of(t * lines, lines), lines)
    fresh = state[here, :] + jnp.sum(red[...], axis=0) / width
    total[...] = fresh
    full[t] = fresh
    for k in reversed(range(1, tb)):
        pltpu.make_async_remote_copy(
            src_ref=total, dst_ref=full.at[t],
            send_sem=send_a.at[0], recv_sem=recv_a.at[k // 4],
            device_id=(d, ts[k]), device_id_type=MESH,
        ).start()

    def update(j):
        fresh = full[j]
        state_out[j] = fresh
        scale = learn_rate / jnp.sqrt(fresh)
        for r in range(lines):
            h, half = r // parts, r % parts
            at = pl.multiple_of((j * each + h) * cols, cols)
            lanes = pl.ds(pl.multiple_of((j * lines + r) * LANES, LANES), LANES)
            step = acc[pl.ds(at, cols), half * LANES:(half + 1) * LANES]
            table_out[:, lanes] = table[:, lanes] - step * scale[r:r + 1, :]

    update(t)
    pltpu.make_async_copy(g_ref.at[:, 0], pair_g.at[:, 0], send_g.at[0]).wait()
    pltpu.make_async_copy(id_ref, pair_i.at[0], send_i.at[0]).wait()
    wait_blocks(got_g, send_g.at[1], chips - 1)
    wait_blocks(got_i, send_i.at[1], chips - 1)
    wait_blocks(red, send_r.at[0], tb - 1)
    for first in range(0, tb, 4):
        wait_blocks(full, recv_a.at[first // 4], 4 if first else 3)
        for k in range(max(first, 1), first + 4):
            update(ts[k])
    wait_blocks(full, send_a.at[0], tb - 1)


def finish_kernel(table_ref, state_ref, table_out, state_out, sems):
    rows = table_ref.shape[1]
    size = rows // PIECES
    copies = [
        pltpu.make_async_copy(
            table_ref.at[:, pl.ds(p * size, size)], table_out.at[:, pl.ds(p * size, size)], sems.at[p]
        )
        for p in range(PIECES)
    ]
    copies.append(pltpu.make_async_copy(state_ref, state_out, sems.at[PIECES]))
    for copy in copies:
        copy.start()
    for copy in copies:
        copy.wait()


def kernel_body(dp, tb, width, gradients, row_ids, table_block, adagrad_state):
    cols, rows = table_block.shape
    count = row_ids.shape[0]
    chips = dp * tb // 2
    his = rows // LO
    lines = rows // tb // LANES
    dma = pltpu.SemaphoreType.DMA
    new_table, new_state = pl.pallas_call(
        functools.partial(exchange_kernel, dp, tb, cols, rows, width),
        name="exchange",
        out_shape=(
            pltpu.VMEM((cols, rows), jnp.float32),
            pltpu.VMEM((tb, lines, LANES), jnp.float32),
        ),
        in_specs=[pl.BlockSpec(memory_space=pl.ANY)] * 4,
        out_specs=(pl.BlockSpec(memory_space=pltpu.VMEM),) * 2,
        scratch_shapes=[
            pltpu.VMEM((his * cols, LO), jnp.float32),
            pltpu.VMEM((tb // 2, 2, cols, count), jnp.bfloat16),
            pltpu.VMEM((2, 1, count), jnp.int32),
            pltpu.VMEM((chips, 2, cols, count), jnp.bfloat16),
            pltpu.VMEM((chips, 2, 1, count), jnp.int32),
            pltpu.VMEM((cols, rows), jnp.float32),
            pltpu.VMEM((tb, lines, LANES), jnp.float32),
            pltpu.VMEM((tb, lines, LANES), jnp.float32),
            pltpu.VMEM((lines, LANES), jnp.float32),
            pltpu.VMEM((tb, lines, LANES), jnp.float32),
            pltpu.VMEM((rows // LANES, LANES), jnp.float32),
            dma((2,)), dma((2,)), dma((1,)), dma((1,)),
            dma((1 + chips // GROUP,)), dma((1 + chips // GROUP,)), dma((1,)), dma((tb // 4,)),
            dma((4,)),
            pltpu.SemaphoreType.REGULAR((1 + len(ready_groups(chips)),)),
        ],
        compiler_params=pltpu.CompilerParams(collective_id=0, has_side_effects=True),
    )(
        gradients.reshape(tb // 2, 2, cols, count),
        row_ids.reshape(1, count),
        adagrad_state.reshape(rows // LANES, LANES),
        table_block,
    )
    new_table, new_state = pl.pallas_call(
        finish_kernel,
        name="finish",
        out_shape=(
            jax.ShapeDtypeStruct((cols, rows), jnp.float32),
            jax.ShapeDtypeStruct((tb, lines, LANES), jnp.float32),
        ),
        in_specs=[pl.BlockSpec(memory_space=pltpu.VMEM)] * 2,
        out_specs=(pl.BlockSpec(memory_space=pl.ANY),) * 2,
        scratch_shapes=[dma((PIECES + 1,))],
    )(
        pltpu.with_memory_space_constraint(new_table, pltpu.VMEM),
        pltpu.with_memory_space_constraint(new_state, pltpu.VMEM),
    )
    return (new_table, new_state.reshape(rows))


def body(dp, tb, gradients, row_ids, table_block, adagrad_state):
    width = gradients.shape[0]
    cols, rows = table_block.shape
    fits = (
        cols % 16 == 0
        and rows % (tb * 8 * LANES) == 0
        and rows % (4 * LO * 4) == 0
        and dp & (dp - 1) == 0
        and tb & (tb - 1) == 0
        and tb % 4 == 0
        and dp * tb % (2 * GROUP) == 0
        and rows // LO <= 256
        and row_ids.shape[0] == LANES
    )
    args = (gradients, row_ids, table_block, adagrad_state)
    if fits:
        return kernel_body(dp, tb, width, *args)
    return plain_body(width, *args)


def solution(mesh):
    in_specs = (P(None, ("dp", "table")), P(("dp", "table")), P("table", "dp"), P("dp"))
    out_specs = (P("table", "dp"), P("dp"))
    run = functools.partial(body, mesh.shape["dp"], mesh.shape["table"])
    return jax.shard_map(run, mesh=mesh, in_specs=in_specs, out_specs=out_specs, check_vma=False)
```

time: 26.3 us -> 24.7 us (0.939)
  Pallas kernels: 25.5 us -> 23.9 us
    pallas_call x1, Pallas kernels: 24.5 us -> 22.9 us  [kernel_body(): pl.pallas_call(functools.partial(exchange_kernel, dp, tb, cols, rows, wid...]
where the time goes in v1:
time: 24.7 us; the launch traced here: 24.6 us
  Pallas kernels  23.9 us (97%)
  between operations  0.64 us (3%)
    pallas_call x1, Pallas kernels, kernel_body(): pl.pallas_call(functools.partial(exchange_kernel, dp, tb, cols, rows, wid...  22.9 us
    pallas_call x1, Pallas kernels, kernel_body(): pl.pallas_call(finish_kernel, name='finish', out_shape=(jax.ShapeDtypeStr...  1.02 us

profile of v1, /device:TPU:0, one launch (start us, length us, event | category | flops | bytes accessed | tf_op | source)
XLA Modules:
  0.0 24.6 jit_solution(11979114503728121674)
XLA Ops:
  0.6 22.9 %exchange.1 = (f32[16,16384]{1,0:T(8,128)S(1)}, f32[16,8,128]{2,1,0:T(8,128)S(1)}) custom-call(bf16[8,2,16,128]{3,2,1,0:T(8,128)(2,1)} %bitcast.4, s32[1,128]{1,0:T(1,128)} %bitcast.6, f32[128,128]{1,0:T(8,128)} %bitcast.5, f32[16,16384]{1,0:T(8,128)} %table_ref.1), custom_call_target="tpu_custom_call" | custom-call | tf_op jit(solution)/shard_map/exchange/pallas_call | solution.py:285
  23.5 1.0 %finish.1 = (f32[16,16384]{1,0:T(8,128)}, f32[16,8,128]{2,1,0:T(8,128)}) custom-call(f32[16,16384]{1,0:T(8,128)S(1)} %get-tuple-element.6.table_ref, f32[16,8,128]{2,1,0:T(8,128)S(1)} %get-tuple-element.7.state_ref), custom_call_target="tpu_custom_call" | custom-call | tf_op jit(solution)/shard_map/finish/pallas_call | solution.py:318

commit v2 on v1

--- a/solution.py
+++ b/solution.py
@@ -12,7 +12,7 @@
 LANES = 128
 GROUP = 4
 READY = 2
-PIECES = 4
+PIECES = 2
 MESH = pl.DeviceIdType.MESH
 
 
@@ -168,8 +168,8 @@
                 send(m)
 
     acc[...] = jnp.zeros_like(acc)
-    got_g[0] = pair_g[spot]
-    got_i[0] = pair_i[...]
+    pltpu.make_async_copy(pair_g.at[spot], got_g.at[0], recv_g.at[1]).start()
+    pltpu.make_async_copy(pair_i, got_i.at[0], recv_i.at[1]).start()
 
     for g, group in enumerate(groups):
         @pl.when(jnp.logical_not(earlier(group)))
@@ -196,11 +196,11 @@
             picked, one_hot, (((1,), (1,)), ((), ())), preferred_element_type=jnp.float32
         )
 
-    for first in range(0, chips, GROUP):
-        count = GROUP if first else GROUP - 1
-        wait_blocks(got_i, recv_i.at[1 + first // GROUP], count)
-        wait_blocks(got_g, recv_g.at[1 + first // GROUP], count)
-        add(range(first, first + GROUP))
+    @pl.loop(0, chips // GROUP)
+    def _(g):
+        wait_blocks(got_i, recv_i.at[1 + g], GROUP)
+        wait_blocks(got_g, recv_g.at[1 + g], GROUP)
+        add([g * GROUP + m for m in range(GROUP)])
 
     for j in range(tb):
         pieces = []

time: 24.7 us -> 23.8 us (0.964)
  Pallas kernels: 23.9 us -> 23 us
    pallas_call x1, Pallas kernels: 22.9 us -> 22 us  [kernel_body(): pl.pallas_call(functools.partial(exchange_kernel, dp, tb, cols, rows, wid...]
where the time goes in v2:
time: 23.8 us; the launch traced here: 23.6 us
  Pallas kernels  23 us (97%)
  between operations  0.64 us (3%)
    pallas_call x1, Pallas kernels, kernel_body(): pl.pallas_call(functools.partial(exchange_kernel, dp, tb, cols, rows, wid...  22 us
    pallas_call x1, Pallas kernels, kernel_body(): pl.pallas_call(finish_kernel, name='finish', out_shape=(jax.ShapeDtypeStr...  1 us

profile of v2, /device:TPU:0, one launch (start us, length us, event | category | flops | bytes accessed | tf_op | source)
XLA Modules:
  0.0 23.6 jit_solution(4185942773869597288)
XLA Ops:
  0.6 22.0 %exchange.1 = (f32[16,16384]{1,0:T(8,128)S(1)}, f32[16,8,128]{2,1,0:T(8,128)S(1)}) custom-call(bf16[8,2,16,128]{3,2,1,0:T(8,128)(2,1)} %bitcast.4, s32[1,128]{1,0:T(1,128)} %bitcast.6, f32[128,128]{1,0:T(8,128)} %bitcast.5, f32[16,16384]{1,0:T(8,128)} %table_ref.1), custom_call_target="tpu_custom_call" | custom-call | tf_op jit(solution)/shard_map/exchange/pallas_call | solution.py:285
  22.6 1.0 %finish.1 = (f32[16,16384]{1,0:T(8,128)}, f32[16,8,128]{2,1,0:T(8,128)}) custom-call(f32[16,16384]{1,0:T(8,128)S(1)} %get-tuple-element.6.table_ref, f32[16,8,128]{2,1,0:T(8,128)S(1)} %get-tuple-element.7.state_ref), custom_call_target="tpu_custom_call" | custom-call | tf_op jit(solution)/shard_map/finish/pallas_call | solution.py:318

commit v3 on v2

--- a/solution.py
+++ b/solution.py
@@ -12,7 +12,7 @@
 LANES = 128
 GROUP = 4
 READY = 2
-PIECES = 2
+PIECES = 4
 MESH = pl.DeviceIdType.MESH
 
 
@@ -59,8 +59,8 @@
 
 def exchange_kernel(
     dp, tb, cols, rows, width,
-    g_ref, id_ref, state_ref, table_ref, table_out, state_out,
-    acc, pair_g, pair_i, got_g, got_i, table, part, red, total, full, state,
+    g_ref, id_ref, state_ref, table_ref, acc, table, state_out,
+    pair_g, pair_i, got_g, got_i, part, red, total, full, state,
     send_g, send_i, send_r, send_a, recv_g, recv_i, recv_r, recv_a, own_sem, ready,
 ):
     d, t = lax.axis_index("dp"), lax.axis_index("table")
@@ -75,6 +75,23 @@
     order = t // 4 * (2 * dp) + d * 2 + lax.rem(spot, 2)
     groups = ready_groups(chips)
     sibling = (d, ts[1])
+    middle = lax.rem(t // 4 + t // 8, 2) == 1
+    far = chips * 3 // 4
+
+    def turns(sequence, near_first):
+        sequence = list(sequence)
+        close = [group for group in sequence if group[0] < chips // 2]
+        cross = [group for group in sequence if chips // 2 <= group[0] < far]
+        long = [group for group in sequence if far <= group[0]]
+        if near_first:
+            first = [(True, group) for group in close]
+            return first + [(middle, group) for group in long] + [(True, group) for group in cross] + [
+                (jnp.logical_not(middle), group) for group in long
+            ]
+        last = [(True, group) for group in close]
+        return [(middle, group) for group in cross] + [(True, group) for group in long] + [
+            (jnp.logical_not(middle), group) for group in cross
+        ] + last
 
     def device(m):
         return ds[m // 2 % dp], ts[m % 2 * 2 + m // (2 * dp) * 4]
@@ -161,8 +178,8 @@
             device_id=to, device_id_type=MESH,
         ).start()
 
-    for group in reversed(groups):
-        @pl.when(earlier(group))
+    for turn, group in turns(reversed(groups), False):
+        @pl.when(jnp.logical_and(earlier(group), turn))
         def _(group=group):
             for m in reversed(group):
                 send(m)
@@ -171,9 +188,9 @@
     pltpu.make_async_copy(pair_g.at[spot], got_g.at[0], recv_g.at[1]).start()
     pltpu.make_async_copy(pair_i, got_i.at[0], recv_i.at[1]).start()
 
-    for g, group in enumerate(groups):
-        @pl.when(jnp.logical_not(earlier(group)))
-        def _(g=g, group=group):
+    for turn, group in turns(groups, True):
+        @pl.when(jnp.logical_and(jnp.logical_not(earlier(group)), turn))
+        def _(g=groups.index(group), group=group):
             pl.semaphore_wait(ready.at[g + 1], len(group))
             for m in group:
                 send(m)
@@ -197,28 +214,34 @@
         )
 
     @pl.loop(0, chips // GROUP)
-    def _(g):
+    def _(turn):
+        half = chips // GROUP // 2
+        quarter = chips // GROUP // 4
+        swap = jnp.where(jnp.logical_and(middle, turn >= half), 1, 0)
+        g = turn + swap * (quarter - 2 * quarter * ((turn - half) // quarter))
         wait_blocks(got_i, recv_i.at[1 + g], GROUP)
         wait_blocks(got_g, recv_g.at[1 + g], GROUP)
         add([g * GROUP + m for m in range(GROUP)])
 
-    for j in range(tb):
+    def part_copy(k):
+        return pltpu.make_async_remote_copy(
+            src_ref=part.at[k], dst_ref=red.at[k],
+            send_sem=send_r.at[0], recv_sem=recv_r.at[0],
+            device_id=(d, ts[k]), device_id_type=MESH,
+        )
+
+    for k in reversed(range(tb)):
         pieces = []
         for h in range(each):
-            at = (j * each + h) * cols
-            piece = acc[at:at + cols, :]
+            at = pl.multiple_of((ts[k] * each + h) * cols, cols)
+            piece = acc[pl.ds(at, cols), :]
             sums = jnp.sum(piece * piece, axis=0, keepdims=True)
             for half in range(parts):
                 pieces.append(sums[:, half * LANES:(half + 1) * LANES])
-        part[j] = jnp.concatenate(pieces, axis=0)
-
-    for k in reversed(range(1, tb)):
-        pltpu.make_async_remote_copy(
-            src_ref=part.at[ts[k]], dst_ref=red.at[k],
-            send_sem=send_r.at[0], recv_sem=recv_r.at[0],
-            device_id=(d, ts[k]), device_id_type=MESH,
-        ).start()
-    red[0] = part[t]
+        part[k] = jnp.concatenate(pieces, axis=0)
+        if k + 1 < tb:
+            part_copy(k + 1).start()
+    red[0] = part[0]
 
     own[2].wait()
     own[3].wait()
@@ -231,46 +254,39 @@
     for k in reversed(range(1, tb)):
         pltpu.make_async_remote_copy(
             src_ref=total, dst_ref=full.at[t],
-            send_sem=send_a.at[0], recv_sem=recv_a.at[k // 4],
+            send_sem=send_a.at[0], recv_sem=recv_a.at[0],
             device_id=(d, ts[k]), device_id_type=MESH,
         ).start()
 
-    def update(j):
-        fresh = full[j]
-        state_out[j] = fresh
-        scale = learn_rate / jnp.sqrt(fresh)
-        for r in range(lines):
-            h, half = r // parts, r % parts
-            at = pl.multiple_of((j * each + h) * cols, cols)
-            lanes = pl.ds(pl.multiple_of((j * lines + r) * LANES, LANES), LANES)
-            step = acc[pl.ds(at, cols), half * LANES:(half + 1) * LANES]
-            table_out[:, lanes] = table[:, lanes] - step * scale[r:r + 1, :]
-
-    update(t)
     pltpu.make_async_copy(g_ref.at[:, 0], pair_g.at[:, 0], send_g.at[0]).wait()
     pltpu.make_async_copy(id_ref, pair_i.at[0], send_i.at[0]).wait()
     wait_blocks(got_g, send_g.at[1], chips - 1)
     wait_blocks(got_i, send_i.at[1], chips - 1)
     wait_blocks(red, send_r.at[0], tb - 1)
-    for first in range(0, tb, 4):
-        wait_blocks(full, recv_a.at[first // 4], 4 if first else 3)
-        for k in range(max(first, 1), first + 4):
-            update(ts[k])
+    wait_blocks(full, recv_a.at[0], tb - 1)
+    state_out[...] = full[...]
     wait_blocks(full, send_a.at[0], tb - 1)
 
 
-def finish_kernel(table_ref, state_ref, table_out, state_out, sems):
-    rows = table_ref.shape[1]
+def finish_kernel(acc, table, state, table_out, state_out, fresh_table, sems):
+    teams, lines, _ = state.shape
+    cols, rows = table.shape
+    parts = LO // LANES
+    each = lines // parts
     size = rows // PIECES
-    copies = [
-        pltpu.make_async_copy(
-            table_ref.at[:, pl.ds(p * size, size)], table_out.at[:, pl.ds(p * size, size)], sems.at[p]
-        )
-        for p in range(PIECES)
-    ]
-    copies.append(pltpu.make_async_copy(state_ref, state_out, sems.at[PIECES]))
-    for copy in copies:
-        copy.start()
+    copies = [pltpu.make_async_copy(state, state_out, sems.at[PIECES])]
+    copies[0].start()
+    for p in range(PIECES):
+        for j in range(p * teams // PIECES, (p + 1) * teams // PIECES):
+            scale = learn_rate / jnp.sqrt(state[j])
+            for r in range(lines):
+                at, half = (j * each + r // parts) * cols, r % parts
+                lanes = slice((j * lines + r) * LANES, (j * lines + r + 1) * LANES)
+                step = acc[at:at + cols, half * LANES:(half + 1) * LANES]
+                fresh_table[:, lanes] = table[:, lanes] - step * scale[r:r + 1, :]
+        there = pl.ds(p * size, size)
+        copies.append(pltpu.make_async_copy(fresh_table.at[:, there], table_out.at[:, there], sems.at[p]))
+        copies[-1].start()
     for copy in copies:
         copy.wait()
 
@@ -282,29 +298,28 @@
     his = rows // LO
     lines = rows // tb // LANES
     dma = pltpu.SemaphoreType.DMA
-    new_table, new_state = pl.pallas_call(
+    row_grad, table, state = pl.pallas_call(
         functools.partial(exchange_kernel, dp, tb, cols, rows, width),
         name="exchange",
         out_shape=(
+            pltpu.VMEM((his * cols, LO), jnp.float32),
             pltpu.VMEM((cols, rows), jnp.float32),
             pltpu.VMEM((tb, lines, LANES), jnp.float32),
         ),
         in_specs=[pl.BlockSpec(memory_space=pl.ANY)] * 4,
-        out_specs=(pl.BlockSpec(memory_space=pltpu.VMEM),) * 2,
+        out_specs=(pl.BlockSpec(memory_space=pltpu.VMEM),) * 3,
         scratch_shapes=[
-            pltpu.VMEM((his * cols, LO), jnp.float32),
             pltpu.VMEM((tb // 2, 2, cols, count), jnp.bfloat16),
             pltpu.VMEM((2, 1, count), jnp.int32),
             pltpu.VMEM((chips, 2, cols, count), jnp.bfloat16),
             pltpu.VMEM((chips, 2, 1, count), jnp.int32),
-            pltpu.VMEM((cols, rows), jnp.float32),
             pltpu.VMEM((tb, lines, LANES), jnp.float32),
             pltpu.VMEM((tb, lines, LANES), jnp.float32),
             pltpu.VMEM((lines, LANES), jnp.float32),
             pltpu.VMEM((tb, lines, LANES), jnp.float32),
             pltpu.VMEM((rows // LANES, LANES), jnp.float32),
             dma((2,)), dma((2,)), dma((1,)), dma((1,)),
-            dma((1 + chips // GROUP,)), dma((1 + chips // GROUP,)), dma((1,)), dma((tb // 4,)),
+            dma((1 + chips // GROUP,)), dma((1 + chips // GROUP,)), dma((1,)), dma((1,)),
             dma((4,)),
             pltpu.SemaphoreType.REGULAR((1 + len(ready_groups(chips)),)),
         ],
@@ -322,12 +337,13 @@
             jax.ShapeDtypeStruct((cols, rows), jnp.float32),
             jax.ShapeDtypeStruct((tb, lines, LANES), jnp.float32),
         ),
-        in_specs=[pl.BlockSpec(memory_space=pltpu.VMEM)] * 2,
+        in_specs=[pl.BlockSpec(memory_space=pltpu.VMEM)] * 3,
         out_specs=(pl.BlockSpec(memory_space=pl.ANY),) * 2,
-        scratch_shapes=[dma((PIECES + 1,))],
+        scratch_shapes=[pltpu.VMEM((cols, rows), jnp.float32), dma((PIECES + 1,))],
     )(
-        pltpu.with_memory_space_constraint(new_table, pltpu.VMEM),
-        pltpu.with_memory_space_constraint(new_state, pltpu.VMEM),
+        pltpu.with_memory_space_constraint(row_grad, pltpu.VMEM),
+        pltpu.with_memory_space_constraint(table, pltpu.VMEM),
+        pltpu.with_memory_space_constraint(state, pltpu.VMEM),
     )
     return (new_table, new_state.reshape(rows))
 
@@ -342,7 +358,7 @@
         and dp & (dp - 1) == 0
         and tb & (tb - 1) == 0
         and tb % 4 == 0
-        and dp * tb % (2 * GROUP) == 0
+        and dp * tb % (8 * GROUP) == 0
         and rows // LO <= 256
         and row_ids.shape[0] == LANES
     )

time: 23.8 us -> 23.3 us (0.979)
  Pallas kernels: 23 us -> 22.5 us
    pallas_call x1, Pallas kernels: 22 us -> 21.5 us  [kernel_body(): pl.pallas_call(functools.partial(exchange_kernel, dp, tb, cols, rows, wid...]
where the time goes in v3:
time: 23.3 us; the launch traced here: 23.2 us
  Pallas kernels  22.5 us (97%)
  between operations  0.64 us (3%)
    pallas_call x1, Pallas kernels, kernel_body(): pl.pallas_call(functools.partial(exchange_kernel, dp, tb, cols, rows, wid...  21.5 us
    pallas_call x1, Pallas kernels, kernel_body(): pl.pallas_call(finish_kernel, name='finish', out_shape=(jax.ShapeDtypeStr...  1.05 us

profile of v3, /device:TPU:0, one launch (start us, length us, event | category | flops | bytes accessed | tf_op | source)
XLA Modules:
  0.0 23.2 jit_solution(1557198374273111530)
XLA Ops:
  0.6 21.5 %exchange.1 = (f32[1024,256]{1,0:T(8,128)S(1)}, f32[16,16384]{1,0:T(8,128)S(1)}, f32[16,8,128]{2,1,0:T(8,128)S(1)}) custom-call(bf16[8,2,16,128]{3,2,1,0:T(8,128)(2,1)} %bitcast.4, s32[1,128]{1,0:T(1,128)} %bitcast.6, f32[128,128]{1,0:T(8,128)} %bitcast.5, f32[16,16384]{1,0:T(8,128)} %table_ref.1), custom_call_target="tpu_custom_call" | custom-call | tf_op jit(solution)/shard_map/exchange/pallas_call | solution.py:301
  22.1 1.0 %finish.1 = (f32[16,16384]{1,0:T(8,128)}, f32[16,8,128]{2,1,0:T(8,128)}) custom-call(f32[1024,256]{1,0:T(8,128)S(1)} %get-tuple-element.7.acc, f32[16,16384]{1,0:T(8,128)S(1)} %get-tuple-element.8.table, f32[16,8,128]{2,1,0:T(8,128)S(1)} %get-tuple-element.9.state), custom_call_target="tpu_custom_call" | custom-call | tf_op jit(solution)/shard_map/finish/pallas_call | solution.py:333

commit v4 on v3

--- a/solution.py
+++ b/solution.py
@@ -66,9 +66,11 @@
     d, t = lax.axis_index("dp"), lax.axis_index("table")
     chips = dp * tb // 2
     his = rows // LO
-    lines = rows // tb // LANES
+    teams, base = tb // 2, tb // 4
+    lines = rows // teams // LANES
     parts = LO // LANES
-    each = his // tb
+    each = his // teams
+    reducer = jnp.logical_and(t >= base, t < base + teams)
     first_row = d * rows
     ts, ds = flips(t, tb), flips(d, dp)
     core, spot = lax.rem(t, 2), t // 2
@@ -223,49 +225,82 @@
         wait_blocks(got_g, recv_g.at[1 + g], GROUP)
         add([g * GROUP + m for m in range(GROUP)])
 
-    def part_copy(k):
-        return pltpu.make_async_remote_copy(
-            src_ref=part.at[k], dst_ref=red.at[k],
-            send_sem=send_r.at[0], recv_sem=recv_r.at[0],
-            device_id=(d, ts[k]), device_id_type=MESH,
-        )
-
-    for k in reversed(range(tb)):
+    planes = teams // 4
+    upper = t // (tb // 2)
+
+    def plane(r):
+        return planes - 1 - r + upper * (2 * r - planes + 1)
+
+    slots = [(r, low) for r in range(planes) for low in reversed(range(4))]
+
+    def team_of(slot):
+        r, low = slots[slot]
+        return plane(r) * 4 + lax.rem(ts[low], 4)
+
+    def send_part(slot):
+        team = team_of(slot)
+
+        @pl.when(team + base != t)
+        def _():
+            pltpu.make_async_remote_copy(
+                src_ref=part.at[slot], dst_ref=red.at[t],
+                send_sem=send_r.at[0], recv_sem=recv_r.at[0],
+                device_id=(d, team + base), device_id_type=MESH,
+            ).start()
+
+    def square(slot):
         pieces = []
         for h in range(each):
-            at = pl.multiple_of((ts[k] * each + h) * cols, cols)
+            at = pl.multiple_of((team_of(slot) * each + h) * cols, cols)
             piece = acc[pl.ds(at, cols), :]
             sums = jnp.sum(piece * piece, axis=0, keepdims=True)
             for half in range(parts):
                 pieces.append(sums[:, half * LANES:(half + 1) * LANES])
-        part[k] = jnp.concatenate(pieces, axis=0)
-        if k + 1 < tb:
-            part_copy(k + 1).start()
-    red[0] = part[0]
+        part[slot] = jnp.concatenate(pieces, axis=0)
+
+    for first in range(0, teams, 4):
+        for slot in range(first, first + 4):
+            square(slot)
+        for slot in range(first, first + 4):
+            send_part(slot)
 
     own[2].wait()
+
+    @pl.when(reducer)
+    def _():
+        mine = t - base
+        red[t] = part[teams - 1]
+        wait_blocks(red, recv_r.at[0], tb - 1)
+        here = pl.ds(pl.multiple_of(mine * lines, lines), lines)
+        fresh = state[here, :] + jnp.sum(red[...], axis=0) / width
+        total[...] = fresh
+        full[mine] = fresh
+        near = tb // 4
+        for k in [*range(2 * near, 3 * near), *range(near, 2 * near), *range(3 * near, tb), *range(1, near)]:
+            pltpu.make_async_remote_copy(
+                src_ref=total, dst_ref=full.at[mine],
+                send_sem=send_a.at[0], recv_sem=recv_a.at[0],
+                device_id=(d, ts[k]), device_id_type=MESH,
+            ).start()
+
     own[3].wait()
-
-    wait_blocks(red, recv_r.at[0], tb - 1)
-    here = pl.ds(pl.multiple_of(t * lines, lines), lines)
-    fresh = state[here, :] + jnp.sum(red[...], axis=0) / width
-    total[...] = fresh
-    full[t] = fresh
-    for k in reversed(range(1, tb)):
-        pltpu.make_async_remote_copy(
-            src_ref=total, dst_ref=full.at[t],
-            send_sem=send_a.at[0], recv_sem=recv_a.at[0],
-            device_id=(d, ts[k]), device_id_type=MESH,
-        ).start()
-
     pltpu.make_async_copy(g_ref.at[:, 0], pair_g.at[:, 0], send_g.at[0]).wait()
     pltpu.make_async_copy(id_ref, pair_i.at[0], send_i.at[0]).wait()
     wait_blocks(got_g, send_g.at[1], chips - 1)
     wait_blocks(got_i, send_i.at[1], chips - 1)
-    wait_blocks(red, send_r.at[0], tb - 1)
-    wait_blocks(full, recv_a.at[0], tb - 1)
+
+    @pl.when(reducer)
+    def _():
+        wait_blocks(red, send_r.at[0], teams - 1)
+        wait_blocks(full, recv_a.at[0], teams - 1)
+        wait_blocks(red, send_a.at[0], tb - 1)
+
+    @pl.when(jnp.logical_not(reducer))
+    def _():
+        wait_blocks(red, send_r.at[0], teams)
+        wait_blocks(full, recv_a.at[0], teams)
+
     state_out[...] = full[...]
-    wait_blocks(full, send_a.at[0], tb - 1)
 
 
 def finish_kernel(acc, table, state, table_out, state_out, fresh_table, sems):
@@ -296,7 +331,8 @@
     count = row_ids.shape[0]
     chips = dp * tb // 2
     his = rows // LO
-    lines = rows // tb // LANES
+    teams = tb // 2
+    lines = rows // teams // LANES
     dma = pltpu.SemaphoreType.DMA
     row_grad, table, state = pl.pallas_call(
         functools.partial(exchange_kernel, dp, tb, cols, rows, width),
@@ -304,7 +340,7 @@
         out_shape=(
             pltpu.VMEM((his * cols, LO), jnp.float32),
             pltpu.VMEM((cols, rows), jnp.float32),
-            pltpu.VMEM((tb, lines, LANES), jnp.float32),
+            pltpu.VMEM((teams, lines, LANES), jnp.float32),
         ),
         in_specs=[pl.BlockSpec(memory_space=pl.ANY)] * 4,
         out_specs=(pl.BlockSpec(memory_space=pltpu.VMEM),) * 3,
@@ -313,10 +349,10 @@
             pltpu.VMEM((2, 1, count), jnp.int32),
             pltpu.VMEM((chips, 2, cols, count), jnp.bfloat16),
             pltpu.VMEM((chips, 2, 1, count), jnp.int32),
-            pltpu.VMEM((tb, lines, LANES), jnp.float32),
+            pltpu.VMEM((teams, lines, LANES), jnp.float32),
             pltpu.VMEM((tb, lines, LANES), jnp.float32),
             pltpu.VMEM((lines, LANES), jnp.float32),
-            pltpu.VMEM((tb, lines, LANES), jnp.float32),
+            pltpu.VMEM((teams, lines, LANES), jnp.float32),
             pltpu.VMEM((rows // LANES, LANES), jnp.float32),
             dma((2,)), dma((2,)), dma((1,)), dma((1,)),
             dma((1 + chips // GROUP,)), dma((1 + chips // GROUP,)), dma((1,)), dma((1,)),
@@ -335,7 +371,7 @@
         name="finish",
         out_shape=(
             jax.ShapeDtypeStruct((cols, rows), jnp.float32),
-            jax.ShapeDtypeStruct((tb, lines, LANES), jnp.float32),
+            jax.ShapeDtypeStruct((teams, lines, LANES), jnp.float32),
         ),
         in_specs=[pl.BlockSpec(memory_space=pltpu.VMEM)] * 3,
         out_specs=(pl.BlockSpec(memory_space=pl.ANY),) * 2,
@@ -357,7 +393,7 @@
         and rows % (4 * LO * 4) == 0
         and dp & (dp - 1) == 0
         and tb & (tb - 1) == 0
-        and tb % 4 == 0
+        and tb % 16 == 0
         and dp * tb % (8 * GROUP) == 0
         and rows // LO <= 256
         and row_ids.shape[0] == LANES

time: 23.3 us -> 23.3 us (level)
  no operation moved by 1% of the time
where the time goes in v4:
time: 23.3 us; the launch traced here: 23.2 us
  Pallas kernels  22.5 us (97%)
  between operations  0.64 us (3%)
    pallas_call x1, Pallas kernels, kernel_body(): pl.pallas_call(functools.partial(exchange_kernel, dp, tb, cols, rows, wid...  21.5 us
    pallas_call x1, Pallas kernels, kernel_body(): pl.pallas_call(finish_kernel, name='finish', out_shape=(jax.ShapeDtypeStr...  1.05 us

profile of v4, /device:TPU:0, one launch (start us, length us, event | category | flops | bytes accessed | tf_op | source)
XLA Modules:
  0.0 23.2 jit_solution(5280863179105588155)
XLA Ops:
  0.6 21.5 %exchange.1 = (f32[1024,256]{1,0:T(8,128)S(1)}, f32[16,16384]{1,0:T(8,128)S(1)}, f32[8,16,128]{2,1,0:T(8,128)S(1)}) custom-call(bf16[8,2,16,128]{3,2,1,0:T(8,128)(2,1)} %bitcast.4, s32[1,128]{1,0:T(1,128)} %bitcast.6, f32[128,128]{1,0:T(8,128)} %bitcast.5, f32[16,16384]{1,0:T(8,128)} %table_ref.1), custom_call_target="tpu_custom_call" | custom-call | tf_op jit(solution)/shard_map/exchange/pallas_call | solution.py:337
  22.1 1.0 %finish.1 = (f32[16,16384]{1,0:T(8,128)}, f32[8,16,128]{2,1,0:T(8,128)}) custom-call(f32[1024,256]{1,0:T(8,128)S(1)} %get-tuple-element.7.acc, f32[16,16384]{1,0:T(8,128)S(1)} %get-tuple-element.8.table, f32[8,16,128]{2,1,0:T(8,128)S(1)} %get-tuple-element.9.state), custom_call_target="tpu_custom_call" | custom-call | tf_op jit(solution)/shard_map/finish/pallas_call | solution.py:369
